TPU v7x, 32 devices: a whole 2x2x4 slice. The times are simulated.
32 devices in a mesh: fsdp: 2 (over core), ctx: 4 (over y, x), tp: 4 (over z).
Axes of the slice: x: 2, y: 2, z: 4, core: 2. Of those that a mesh axis runs over, the one named last changes fastest.
Arguments:
- x_prompt: bfloat16 [2, 1024, 1024], P('fsdp', 'ctx'), may hold values from -6 to 6
- x_cont: bfloat16 [2, 12, 256, 1024], P('fsdp', 'ctx'), may hold values from -6 to 6
- cont_start: int32 [2, 12], P('fsdp', 'ctx'), may hold values from 512 to 1024
- w_qkv: bfloat16 [1024, 3, 1024], P(('fsdp', 'ctx'), None, 'tp'), may hold values from -0.1875 to 0.1875
- qkv_bias: bfloat16 [3, 1024], P(None, 'tp'), may hold values from -3 to 3
- w_dense: bfloat16 [1024, 1024], P('tp', ('fsdp', 'ctx')), may hold values from -0.75 to 0.75
- dense_bias: bfloat16 [1024], P(('fsdp', 'ctx')), may hold values from -3 to 3
- w_fc1: bfloat16 [1024, 4096], P(('fsdp', 'ctx'), 'tp'), may hold values from -0.1875 to 0.1875
- fc1_bias: bfloat16 [4096], P('tp'), may hold values from -3 to 3
- w_fc2: bfloat16 [4096, 1024], P('tp', ('fsdp', 'ctx')), may hold values from -0.09375 to 0.09375
- fc2_bias: bfloat16 [1024], P(('fsdp', 'ctx')), may hold values from -3 to 3
- ln1_gain: bfloat16 [1024], P(('fsdp', 'ctx')), may hold values from 0.099609375 to 1.8984375
- ln1_bias: bfloat16 [1024], P(('fsdp', 'ctx')), may hold values from -2 to 2
- ln2_gain: bfloat16 [1024], P(('fsdp', 'ctx')), may hold values from 0.099609375 to 1.8984375
- ln2_bias: bfloat16 [1024], P(('fsdp', 'ctx')), may hold values from -2 to 2
- dy_prompt: bfloat16 [2, 1024, 1024], P('fsdp', 'ctx'), may hold values from -6 to 6
- dy_cont: bfloat16 [2, 12, 256, 1024], P('fsdp', 'ctx'), may hold values from -6 to 6
Outputs:
- y_prompt: float32 [2, 1024, 1024], P('fsdp', 'ctx')
- y_cont: float32 [2, 12, 256, 1024], P('fsdp', 'ctx')
- dx_prompt: float32 [2, 1024, 1024], P('fsdp', 'ctx')
- dx_cont: float32 [2, 12, 256, 1024], P('fsdp', 'ctx')
- d_w_qkv: float32 [1024, 3, 1024], P(('fsdp', 'ctx'), None, 'tp')
- d_qkv_bias: float32 [3, 1024], P(None, 'tp')
- d_w_dense: float32 [1024, 1024], P('tp', ('fsdp', 'ctx'))
- d_dense_bias: float32 [1024], P(('fsdp', 'ctx'))
- d_w_fc1: float32 [1024, 4096], P(('fsdp', 'ctx'), 'tp')
- d_fc1_bias: float32 [4096], P('tp')
- d_w_fc2: float32 [4096, 1024], P('tp', ('fsdp', 'ctx'))
- d_fc2_bias: float32 [1024], P(('fsdp', 'ctx'))
- d_ln1_gain: float32 [1024], P(('fsdp', 'ctx'))
- d_ln1_bias: float32 [1024], P(('fsdp', 'ctx'))
- d_ln2_gain: float32 [1024], P(('fsdp', 'ctx'))
- d_ln2_bias: float32 [1024], P(('fsdp', 'ctx'))
Inputs may be any that keep to these rules, and one draw needn't show every extreme that they name: `cont_start`: a continuation follows the prompt tokens before its first position.
All inputs are finite; a program needn't handle non-finite values.
Results may differ from a plain program's by a relative error of at most 0.012.
Values may be sent and summed in bfloat16 or wider, within the bound.
A program may use at most 192 MiB of HBM per device.

v0:
```python
import jax
import jax.numpy as jnp
from jax import lax
from jax.sharding import PartitionSpec as P

HD = 64
ROT = 16
EPS = 1e-05


def layer_norm(inputs, norm_gain, norm_shift):
    row_mean = jnp.mean(inputs, axis=-1, keepdims=True)
    centered = inputs - row_mean
    variance = jnp.mean(centered * centered, axis=-1, keepdims=True)
    return centered * lax.rsqrt(variance + EPS) * norm_gain + norm_shift


def norm_pair(inputs, gain_one, shift_one, gain_two, shift_two):
    return (layer_norm(inputs, gain_one, shift_one), layer_norm(inputs, gain_two, shift_two))


def exact_gelu(values):
    return jax.nn.gelu(values, approximate=False)


def rotary_tables(positions):
    freq_index = jnp.arange(ROT // 2).astype(jnp.float32)
    inverse = jnp.power(10000.0, -2.0 * freq_index / ROT)
    phase = positions.astype(jnp.float32)[..., None] * inverse
    cos_half = jnp.cos(phase)
    sin_half = jnp.sin(phase)
    return (
        jnp.concatenate([cos_half, cos_half], axis=-1),
        jnp.concatenate([sin_half, sin_half], axis=-1),
    )


def rotate(inputs, cos_t, sin_t):
    leading = inputs[..., :ROT]
    half_rot = ROT // 2
    turned = jnp.concatenate([-leading[..., half_rot:], leading[..., :half_rot]], axis=-1)
    return jnp.concatenate([leading * cos_t + turned * sin_t, inputs[..., ROT:]], axis=-1)


def masked_scores(
    queries, all_keys, key_limit, query_slot, query_offs, prompt_len, key_slot, key_offs
):
    raw_scores = jnp.einsum("qhd,khd->hqk", queries, all_keys, preferred_element_type=jnp.float32)
    key_index = jnp.arange(all_keys.shape[0], dtype=jnp.int32)
    near_keys = key_index[None, :] < key_limit[:, None]
    own_keys = (key_slot[None, :] == query_slot[:, None]) & (
        key_offs[None, :] <= query_offs[:, None]
    )
    allowed = jnp.where((key_index < prompt_len)[None, :], near_keys, own_keys)
    return jnp.where(allowed[None], raw_scores * 0.125, -1e30)


def on_device(
    x_prompt,
    x_cont,
    cont_start,
    w_qkv,
    qkv_bias,
    w_dense,
    dense_bias,
    w_fc1,
    fc1_bias,
    w_fc2,
    fc2_bias,
    ln1_gain,
    ln1_bias,
    ln2_gain,
    ln2_bias,
    dy_prompt,
    dy_cont,
):
    gathered = (
        lax.all_gather(w_qkv, ("fsdp", "ctx"), axis=0, tiled=True),
        lax.all_gather(w_dense, ("fsdp", "ctx"), axis=1, tiled=True),
        lax.all_gather(w_fc1, ("fsdp", "ctx"), axis=0, tiled=True),
        lax.all_gather(w_fc2, ("fsdp", "ctx"), axis=1, tiled=True),
        lax.all_gather(dense_bias, ("fsdp", "ctx"), axis=0, tiled=True),
        lax.all_gather(fc2_bias, ("fsdp", "ctx"), axis=0, tiled=True),
        lax.all_gather(ln1_gain, ("fsdp", "ctx"), axis=0, tiled=True),
        lax.all_gather(ln1_bias, ("fsdp", "ctx"), axis=0, tiled=True),
        lax.all_gather(ln2_gain, ("fsdp", "ctx"), axis=0, tiled=True),
        lax.all_gather(ln2_bias, ("fsdp", "ctx"), axis=0, tiled=True),
    )
    qkv_full, dense_full, up_full, down_full = (gathered[0], gathered[1], gathered[2], gathered[3])
    dense_shift = gathered[4].astype(jnp.float32)
    down_shift = gathered[5].astype(jnp.float32)
    gain_one = gathered[6].astype(jnp.float32)
    shift_one = gathered[7].astype(jnp.float32)
    gain_two = gathered[8].astype(jnp.float32)
    shift_two = gathered[9].astype(jnp.float32)
    p_rows = x_prompt.shape[1]
    cont_count = x_cont.shape[1]
    cont_len = x_cont.shape[2]
    model_width = x_prompt.shape[2]
    row_count = p_rows + cont_count * cont_len
    prompt_len = p_rows * lax.axis_size("ctx")
    local_cols = qkv_full.shape[2]
    head_count = local_cols // HD
    piece_index = lax.axis_index("ctx")
    inputs = jnp.concatenate(
        [x_prompt[0], x_cont[0].reshape(cont_count * cont_len, model_width)], axis=0
    ).astype(jnp.float32)
    offsets = jnp.arange(cont_len, dtype=jnp.int32)
    prompt_pos = piece_index * p_rows + jnp.arange(p_rows, dtype=jnp.int32)
    starts = cont_start[0]
    cont_pos = (starts[:, None] + offsets[None, :]).reshape(cont_count * cont_len)
    positions = jnp.concatenate([prompt_pos, cont_pos])
    key_limit = jnp.concatenate([prompt_pos + 1, jnp.repeat(starts, cont_len)])
    own_slot = jnp.repeat(jnp.arange(cont_count, dtype=jnp.int32), cont_len)
    own_offs = jnp.tile(offsets, cont_count)
    query_slot = jnp.concatenate([jnp.full((p_rows,), -1, jnp.int32), own_slot])
    query_offs = jnp.concatenate([jnp.zeros((p_rows,), jnp.int32), own_offs])
    key_slot = jnp.concatenate([jnp.full((prompt_len,), -1, jnp.int32), own_slot])
    key_offs = jnp.concatenate([jnp.zeros((prompt_len,), jnp.int32), own_offs])
    cos_t, sin_t = rotary_tables(positions)
    cos_t = cos_t[:, None, :]
    sin_t = sin_t[:, None, :]
    norm_one, norm_two = norm_pair(inputs, gain_one, shift_one, gain_two, shift_two)
    ln_one = norm_one.astype(jnp.bfloat16)
    ln_two = norm_two.astype(jnp.bfloat16)
    qkv_flat = qkv_full.reshape(model_width, 3 * local_cols)
    projected = jnp.dot(ln_one, qkv_flat, preferred_element_type=jnp.float32) + qkv_bias.reshape(
        3 * local_cols
    ).astype(jnp.float32)
    projected = projected.reshape(row_count, 3, head_count, HD)
    queries = rotate(projected[:, 0], cos_t, sin_t).astype(jnp.bfloat16)
    keys_own = rotate(projected[:, 1], cos_t, sin_t).astype(jnp.bfloat16)
    values_own = projected[:, 2].astype(jnp.bfloat16)
    prompt_keys, prompt_values = (
        lax.all_gather(keys_own[:p_rows].reshape(p_rows, local_cols), "ctx", axis=0, tiled=True),
        lax.all_gather(values_own[:p_rows].reshape(p_rows, local_cols), "ctx", axis=0, tiled=True),
    )
    all_keys = jnp.concatenate(
        [prompt_keys.reshape(prompt_len, head_count, HD), keys_own[p_rows:]], axis=0
    )
    all_values = jnp.concatenate(
        [prompt_values.reshape(prompt_len, head_count, HD), values_own[p_rows:]], axis=0
    )
    scores = masked_scores(
        queries, all_keys, key_limit, query_slot, query_offs, prompt_len, key_slot, key_offs
    )
    highest = jnp.max(scores, axis=-1, keepdims=True)
    log_total = highest + jnp.log(jnp.sum(jnp.exp(scores - highest), axis=-1, keepdims=True))
    probs_low = jnp.exp(scores - log_total).astype(jnp.bfloat16)
    attended = jnp.einsum("hqk,khd->qhd", probs_low, all_values, preferred_element_type=jnp.float32)
    attended_low = attended.reshape(row_count, local_cols).astype(jnp.bfloat16)
    attn_part = jnp.dot(attended_low, dense_full, preferred_element_type=jnp.float32)
    hidden = jnp.dot(ln_two, up_full, preferred_element_type=jnp.float32) + fc1_bias.astype(
        jnp.float32
    )
    active_low = exact_gelu(hidden).astype(jnp.bfloat16)
    mlp_part = jnp.dot(active_low, down_full, preferred_element_type=jnp.float32)
    attn_total = lax.psum(attn_part, "tp")
    mlp_total = lax.psum(mlp_part.astype(jnp.bfloat16), "tp").astype(jnp.float32)
    mixed = attn_total + mlp_total
    output = inputs + mixed + dense_shift + down_shift
    again = (
        lax.all_gather(w_qkv, ("fsdp", "ctx"), axis=0, tiled=True),
        lax.all_gather(w_dense, ("fsdp", "ctx"), axis=1, tiled=True),
        lax.all_gather(w_fc1, ("fsdp", "ctx"), axis=0, tiled=True),
        lax.all_gather(w_fc2, ("fsdp", "ctx"), axis=1, tiled=True),
    )
    qkv_flat = again[0].reshape(model_width, 3 * local_cols)
    dense_full, up_full, down_full = (again[1], again[2], again[3])
    grad_out = jnp.concatenate(
        [dy_prompt[0], dy_cont[0].reshape(cont_count * cont_len, model_width)], axis=0
    )
    grad_dense = jnp.dot(attended_low.T, grad_out, preferred_element_type=jnp.float32)
    grad_down = jnp.dot(active_low.T, grad_out, preferred_element_type=jnp.float32)
    grad_shift = jnp.sum(grad_out.astype(jnp.float32), axis=0)
    grad_attended = (
        jnp.dot(grad_out, dense_full.T, preferred_element_type=jnp.float32)
        .astype(jnp.bfloat16)
        .reshape(row_count, head_count, HD)
    )
    scores = masked_scores(
        queries, all_keys, key_limit, query_slot, query_offs, prompt_len, key_slot, key_offs
    )
    probs = jnp.exp(scores - log_total)
    probs_low = probs.astype(jnp.bfloat16)
    grad_probs = jnp.einsum(
        "qhd,khd->hqk", grad_attended, all_values, preferred_element_type=jnp.float32
    )
    inner = jnp.sum(probs * grad_probs, axis=-1, keepdims=True)
    grad_scores = (probs * (grad_probs - inner)).astype(jnp.bfloat16)
    grad_queries = (
        jnp.einsum("hqk,khd->qhd", grad_scores, all_keys, preferred_element_type=jnp.float32)
        * 0.125
    )
    grad_keys = (
        jnp.einsum("hqk,qhd->khd", grad_scores, queries, preferred_element_type=jnp.float32) * 0.125
    )
    grad_values = jnp.einsum(
        "hqk,qhd->khd", probs_low, grad_attended, preferred_element_type=jnp.float32
    )
    prompt_key_grads, prompt_value_grads = (
        lax.psum_scatter(
            grad_keys[:prompt_len].reshape(prompt_len, local_cols),
            "ctx",
            scatter_dimension=0,
            tiled=True,
        ),
        lax.psum_scatter(
            grad_values[:prompt_len].reshape(prompt_len, local_cols),
            "ctx",
            scatter_dimension=0,
            tiled=True,
        ),
    )
    grad_keys = jnp.concatenate(
        [prompt_key_grads.reshape(p_rows, head_count, HD), grad_keys[prompt_len:]], axis=0
    )
    grad_values = jnp.concatenate(
        [prompt_value_grads.reshape(p_rows, head_count, HD), grad_values[prompt_len:]], axis=0
    )
    grad_projected = jnp.stack(
        [rotate(grad_queries, cos_t, -sin_t), rotate(grad_keys, cos_t, -sin_t), grad_values], axis=1
    )
    grad_proj_low = grad_projected.reshape(row_count, 3 * local_cols).astype(jnp.bfloat16)
    grad_qkv = jnp.dot(ln_one.T, grad_proj_low, preferred_element_type=jnp.float32).reshape(
        model_width, 3, local_cols
    )
    grad_qkv_bias = jnp.sum(grad_proj_low.astype(jnp.float32), axis=0).reshape(3, local_cols)
    grad_norm_one = jnp.dot(grad_proj_low, qkv_flat.T, preferred_element_type=jnp.float32)
    grad_active = jnp.dot(grad_out, down_full.T, preferred_element_type=jnp.float32)
    gelu_back = jax.vjp(exact_gelu, hidden)[1]
    grad_hidden_low = gelu_back(grad_active)[0].astype(jnp.bfloat16)
    grad_up = jnp.dot(ln_two.T, grad_hidden_low, preferred_element_type=jnp.float32)
    grad_up_bias = jnp.sum(grad_hidden_low.astype(jnp.float32), axis=0)
    grad_norm_two = jnp.dot(grad_hidden_low, up_full.T, preferred_element_type=jnp.float32)
    norm_back = jax.vjp(norm_pair, inputs, gain_one, shift_one, gain_two, shift_two)[1]
    full_one = lax.psum(grad_norm_one, "tp")
    full_two = lax.psum(grad_norm_two, "tp")
    grad_in, grad_gain_one, grad_shift_one, grad_gain_two, grad_shift_two = norm_back(
        (full_one, full_two)
    )
    grad_inputs = grad_in + grad_out.astype(jnp.float32)
    owned = (
        lax.psum_scatter(grad_qkv, ("fsdp", "ctx"), scatter_dimension=0, tiled=True),
        lax.psum_scatter(grad_dense, ("fsdp", "ctx"), scatter_dimension=1, tiled=True),
        lax.psum_scatter(grad_up, ("fsdp", "ctx"), scatter_dimension=0, tiled=True),
        lax.psum_scatter(grad_down, ("fsdp", "ctx"), scatter_dimension=1, tiled=True),
        lax.psum_scatter(grad_shift, ("fsdp", "ctx"), scatter_dimension=0, tiled=True),
        lax.psum_scatter(grad_gain_one, ("fsdp", "ctx"), scatter_dimension=0, tiled=True),
        lax.psum_scatter(grad_shift_one, ("fsdp", "ctx"), scatter_dimension=0, tiled=True),
        lax.psum_scatter(grad_gain_two, ("fsdp", "ctx"), scatter_dimension=0, tiled=True),
        lax.psum_scatter(grad_shift_two, ("fsdp", "ctx"), scatter_dimension=0, tiled=True),
    )
    bias_qkv_total, bias_up_total = lax.psum((grad_qkv_bias, grad_up_bias), ("fsdp", "ctx"))
    y_prompt = output[:p_rows][None]
    y_cont = output[p_rows:].reshape(1, cont_count, cont_len, model_width)
    dx_prompt = grad_inputs[:p_rows][None]
    dx_cont = grad_inputs[p_rows:].reshape(1, cont_count, cont_len, model_width)
    return (
        y_prompt,
        y_cont,
        dx_prompt,
        dx_cont,
        owned[0],
        bias_qkv_total,
        owned[1],
        owned[4],
        owned[2],
        bias_up_total,
        owned[3],
        owned[4],
        owned[5],
        owned[6],
        owned[7],
        owned[8],
    )


def solution(mesh):
    placed = (
        P("fsdp", "ctx", None),
        P("fsdp", "ctx", None, None),
        P("fsdp", "ctx"),
        P(("fsdp", "ctx"), None, "tp"),
        P(None, "tp"),
        P("tp", ("fsdp", "ctx")),
        P(("fsdp", "ctx")),
        P(("fsdp", "ctx"), "tp"),
        P("tp"),
        P("tp", ("fsdp", "ctx")),
        P(("fsdp", "ctx")),
        P(("fsdp", "ctx")),
        P(("fsdp", "ctx")),
        P(("fsdp", "ctx")),
        P(("fsdp", "ctx")),
        P("fsdp", "ctx", None),
        P("fsdp", "ctx", None, None),
    )
    return jax.shard_map(
        on_device,
        mesh=mesh,
        in_specs=placed,
        out_specs=(
            P("fsdp", "ctx", None),
            P("fsdp", "ctx", None, None),
            P("fsdp", "ctx", None),
            P("fsdp", "ctx", None, None),
            P(("fsdp", "ctx"), None, "tp"),
            P(None, "tp"),
            P("tp", ("fsdp", "ctx")),
            P(("fsdp", "ctx")),
            P(("fsdp", "ctx"), "tp"),
            P("tp"),
            P("tp", ("fsdp", "ctx")),
            P(("fsdp", "ctx")),
            P(("fsdp", "ctx")),
            P(("fsdp", "ctx")),
            P(("fsdp", "ctx")),
            P(("fsdp", "ctx")),
        ),
        check_vma=False,
    )
```

profile of v0, /device:TPU:0, one launch (start us, length us, event | category | flops | bytes accessed | tf_op | source)
XLA Modules:
  0.0 1037.2 jit_solution(66057958732764653)
XLA Ops:
  7.3 1.9 copy.36
  13.8 1.9 convert_reduce_fusion
  15.7 1.7 fusion.19
  18.0 14.7 %all-gather = bf16[8,1,128]{2,1,0:T(2,128)(2,1)S(1)} all-gather(bf16[1,1,128]{2,1,0:T(2,128)(2,1)S(1)} %bitcast.150), channel_id=1, replica_groups=mesh['fsdp'=2,'ctx'=4,'tp'=4] {'fsdp','ctx'}, dimensions={0}, use_global_device_ids=true | all-gather | bytes 2304 | tf_op jit(solution)/shard_map/all_gather | solution.py:84
  32.7 13.2 %all-gather.1 = bf16[8,1,128]{2,1,0:T(2,128)(2,1)S(1)} all-gather(bf16[1,1,128]{2,1,0:T(2,128)(2,1)S(1)} %bitcast.151), channel_id=1, replica_groups=mesh['fsdp'=2,'ctx'=4,'tp'=4] {'fsdp','ctx'}, dimensions={0}, use_global_device_ids=true | all-gather | bytes 2304 | tf_op jit(solution)/shard_map/all_gather | solution.py:85
  48.1 25.5 %all_gather.45 = bf16[256,1024]{1,0:T(8,128)(2,1)S(1)} all-gather(bf16[256,128]{1,0:T(8,128)(2,1)S(1)} %copy-done.22), channel_id=1, replica_groups=mesh['fsdp'=2,'ctx'=4,'tp'=4] {'fsdp','ctx'}, dimensions={1}, use_global_device_ids=true | all-gather | bytes 589824 | tf_op jit(solution)/shard_map/all_gather | solution.py:79
  73.6 12.2 %all-gather.2 = bf16[8,1,128]{2,1,0:T(2,128)(2,1)S(1)} all-gather(bf16[1,1,128]{2,1,0:T(2,128)(2,1)S(1)} %bitcast.153), channel_id=1, replica_groups=mesh['fsdp'=2,'ctx'=4,'tp'=4] {'fsdp','ctx'}, dimensions={0}, use_global_device_ids=true | all-gather | bytes 2304 | tf_op jit(solution)/shard_map/all_gather | solution.py:86
  85.8 13.8 %all-gather.3 = bf16[8,1,128]{2,1,0:T(2,128)(2,1)S(1)} all-gather(bf16[1,1,128]{2,1,0:T(2,128)(2,1)S(1)} %bitcast.154), channel_id=1, replica_groups=mesh['fsdp'=2,'ctx'=4,'tp'=4] {'fsdp','ctx'}, dimensions={0}, use_global_device_ids=true | all-gather | bytes 2304 | tf_op jit(solution)/shard_map/all_gather | solution.py:87
  100.9 2.6 convolution_convert_fusion.2
  103.5 3.9 fusion.2
  107.4 3.6 convolution_add_fusion
  111.9 12.9 %all_gather.44 = bf16[1024,256]{0,1:T(8,128)(2,1)S(1)} all-gather(bf16[256,256]{0,1:T(8,128)(2,1)S(1)} %bitcast.131), channel_id=1, replica_groups=mesh['fsdp'=2,'ctx'=4,'tp'=4] {'ctx'}, dimensions={0}, use_global_device_ids=true | all-gather | bytes 655360 | tf_op jit(solution)/shard_map/all_gather | solution.py:135
  124.8 12.9 %fusion = (f32[4,1024]{1,0:T(4,128)S(1)}, f32[4,1024,1792]{2,1,0:T(8,128)}) fusion(pred[1024,1792]{1,0:T(8,128)(4,1)S(1)} %fusion.2, bf16[1024,4,48]{0,2,1:T(8,128)(2,1)S(1)} %slice.216, bf16[1024,4,16]{0,2,1:T(8,128)(2,1)S(1)} %get-tuple-element.57, bf16[1024,4,64]{0,2,1:T(8,128)(2,1)S(1)} %bitcast.123, bf16[1024,4,48]{0,2,1:T(8,128)(2,1)S(1)} %slice.217, ...), kind=kOutput, calls=%fused_computation.5 | convolution fusion | flops 966717440 | bytes 32784384 | tf_op jit(solution)/shard_map/qhd,khd->hqk/dot_general | solution.py:48
  137.6 13.8 %exponential_reduce_fusion = f32[4,1024]{1,0:T(4,128)S(1)} fusion(f32[4,1024,1792]{2,1,0:T(8,128)} %get-tuple-element.66, f32[4,1024]{1,0:T(4,128)S(1)} %get-tuple-element.65, pred[1024,1792]{1,0:T(8,128)(4,1)S(1)} %fusion.2), kind=kLoop, calls=%fused_computation.3 | loop fusion | flops 29356032 | bytes 31227904 | tf_op jit(solution)/shard_map/reduce_sum | solution.py:148
  151.4 12.7 %all_gather.43 = bf16[1024,256]{0,1:T(8,128)(2,1)S(1)} all-gather(bf16[256,256]{0,1:T(8,128)(2,1)S(1)} %bitcast.132), channel_id=1, replica_groups=mesh['fsdp'=2,'ctx'=4,'tp'=4] {'ctx'}, dimensions={0}, use_global_device_ids=true | all-gather | bytes 655360 | tf_op jit(solution)/shard_map/all_gather | solution.py:136
  164.2 22.0 %multiply_reduce_fusion = (f32[4,1024]{1,0:T(4,128)S(1)}, f32[4,1024,1792]{2,1,0:T(8,128)}) fusion(f32[4,1024,1792]{2,1,0:T(8,128)} %get-tuple-element.66, f32[4,1024]{1,0:T(4,128)S(1)} %log_add_fusion, pred[1024,1792]{1,0:T(8,128)(4,1)S(1)} %fusion.2, bf16[1024,4,64]{0,2,1:T(8,128)(2,1)S(1)} %bitcast.129, bf16[768,4,64]{0,2,1:T(8,128)(2,1)S(1)} %slice_bitcast_fusion.4, ...), kind=kOutput, calls=%fused_computation.1 | convolution fusion | flops 978055168 | bytes 62029824 | tf_op jit(solution)/shard_map/qhd,khd->hqk/dot_general | solution.py:186
  186.2 24.6 %multiply_convert_fusion = bf16[4,1024,1792]{2,1,0:T(8,128)(2,1)} fusion(f32[4,1024,1792]{2,1,0:T(8,128)} %get-tuple-element.69, f32[4,1024,1792]{2,1,0:T(8,128)} %get-tuple-element.66, f32[4,1024]{1,0:T(4,128)S(1)} %get-tuple-element.68, f32[4,1024]{1,0:T(4,128)S(1)} %log_add_fusion, pred[1024,1792]{1,0:T(8,128)(4,1)S(1)} %fusion.2), kind=kLoop, calls=%fused_computation | loop fusion | flops 44040192 | bytes 75268096 | tf_op jit(solution)/shard_map/convert_element_type | solution.py:190
  210.8 7.8 fusion.30
  220.7 12.7 %convolution_bitcast_fusion = f32[1792,4,64]{0,2,1:T(8,128)S(1)} fusion(bf16[1024,4,64]{0,2,1:T(8,128)(2,1)S(1)} %bitcast.130, f32[4,1024,1792]{2,1,0:T(8,128)} %get-tuple-element.66, f32[4,1024]{1,0:T(4,128)S(1)} %log_add_fusion, pred[1024,1792]{1,0:T(8,128)(4,1)S(1)} %fusion.2), kind=kOutput, calls=%fused_computation.58 | convolution fusion | flops 968884224 | bytes 33570816 | tf_op jit(solution)/shard_map/hqk,qhd->khd/dot_general | solution.py:198
  235.3 9.7 fusion.35
  246.9 14.3 %convolution_convert_fusion.1 = bf16[4,64,1024]{2,1,0:T(8,128)(2,1)} fusion(bf16[768,4,64]{0,2,1:T(8,128)(2,1)} %copy-done.13, bf16[1024,4,64]{0,2,1:T(8,128)(2,1)} %bitcast.117, f32[4,1024,1792]{2,1,0:T(8,128)} %get-tuple-element.66, f32[4,1024]{1,0:T(4,128)S(1)} %log_add_fusion, pred[1024,1792]{1,0:T(8,128)(4,1)S(1)} %fusion.2), kind=kOutput, calls=%fused_computation.75 | convolution fusion | flops 970981376 | bytes 32653312 | tf_op jit(solution)/shard_map/hqk,khd->qhd/dot_general | solution.py:150
  261.2 4.0 fusion.78
  265.5 16.0 %multiply_convert_fusion.1 = (bf16[1024,1024]{1,0:T(8,128)(2,1)}, f32[1024,1024]{1,0:T(8,128)}, f32[1024,1024]{1,0:T(8,128)}) fusion(f32[1024]{0:T(1024)S(1)} %copy-done.26, bf16[1024,1024]{1,0:T(8,128)(2,1)} %all-gather.12.cloned.1.call-done, f32[1024]{0:T(1024)S(1)} %bitcast.148, f32[1024]{0:T(1024)S(1)} %bitcast.139, f32[1024]{0:T(1024)S(1)} %fusion.55, ...), kind=kOutput, calls=%fused_computation.41 | convolution fusion | flops 2226126848 | bytes 14700544 | tf_op jit(solution)/shard_map/dot_general | solution.py:153
  281.5 9.1 convert_reduce_fusion.2
  292.0 4.4 fusion.79
  298.3 1.8 fusion.38
  300.2 5.3 reduce-scatter.9.cloned.1.call-done
  306.7 1.3 convert_reduce_fusion.3
  309.2 3.8 fusion.80
  313.4 6.0 convolution_convert_fusion
  319.5 3.3 fusion.73
  322.8 5.3 fusion.31
  328.2 6.2 fusion.64
  334.5 6.4 fusion.72
  341.5 13.7 %all-gather.4 = bf16[8,1,128]{2,1,0:T(2,128)(2,1)S(1)} all-gather(bf16[1,1,128]{2,1,0:T(2,128)(2,1)S(1)} %bitcast.155), channel_id=1, replica_groups=mesh['fsdp'=2,'ctx'=4,'tp'=4] {'fsdp','ctx'}, dimensions={0}, use_global_device_ids=true | all-gather | bytes 2304 | tf_op jit(solution)/shard_map/all_gather | solution.py:82
  355.2 13.4 %all-gather.5 = bf16[8,1,128]{2,1,0:T(2,128)(2,1)S(1)} all-gather(bf16[1,1,128]{2,1,0:T(2,128)(2,1)S(1)} %bitcast.156), channel_id=1, replica_groups=mesh['fsdp'=2,'ctx'=4,'tp'=4] {'fsdp','ctx'}, dimensions={0}, use_global_device_ids=true | all-gather | bytes 2304 | tf_op jit(solution)/shard_map/all_gather | solution.py:83
  369.8 370.8 %all-reduce.16.cloned.1.call-done = (f32[1024,1024]{1,0:T(8,128)}, f32[1024,1024]{1,0:T(8,128)}, f32[1024,1024]{1,0:T(8,128)}) async-done(((f32[1024,1024]{1,0:T(8,128)}, f32[1024,1024]{1,0:T(8,128)}, f32[1024,1024]{1,0:T(8,128)}), (f32[1024,1024]{1,0:T(8,128)}, f32[1024,1024]{1,0:T(8,128)}, f32[1024,1024]{1,0:T(8,128)})) %all-reduce.16.cloned.1.call-update) | async-done | bytes 12582928 | tf_op jit(solution)/shard_map/psum | solution.py:158
  740.7 4.7 fusion.76
  745.4 83.7 %all-reduce.14.cloned.1.call-done = bf16[1024,1024]{1,0:T(8,128)(2,1)} async-done(((bf16[1024,1024]{1,0:T(8,128)(2,1)}), bf16[1024,1024]{1,0:T(8,128)(2,1)}) %all-reduce.14.cloned.1.call-update) | async-done | bytes 2097168 | tf_op jit(solution)/shard_map/psum | solution.py:159
  829.1 9.3 fusion.18
  838.4 5.4 convert_reduce_fusion.1
  843.8 26.6 %all-reduce.9 = (f32[3,256]{1,0:T(4,128)}, f32[1024]{0:T(1024)S(1)}, f32[1024]{0:T(1024)}, f32[1024]{0:T(1024)S(1)}, f32[1024]{0:T(1024)S(1)}, /*index=5*/f32[1024]{0:T(1024)S(1)}, f32[1024]{0:T(1024)S(1)}) all-reduce(f32[3,256]{1,0:T(4,128)S(1)} %reshape.336, ...), channel_id=1, replica_groups=mesh['fsdp'=2,'ctx'=4,'tp'=4] {'fsdp','ctx'}, use_global_device_ids=true, to_apply=%region_17.18 | all-reduce | flops 6912 | bytes 55296 | tf_op jit(solution)/shard_map/psum | solution.py:254
  872.8 4.0 slice.168
  876.8 1.9 slice.152
  878.7 2.3 slice_bitcast_fusion
  882.0 36.9 %reduce-scatter.11.cloned.1.call-done = f32[128,3,256]{2,0,1:T(8,128)} async-done(((f32[1024,3,256]{2,0,1:T(8,128)}), f32[128,3,256]{2,0,1:T(8,128)}) %reduce-scatter.11.cloned.1.call-update) | async-done | bytes 393232 | tf_op jit(solution)/shard_map/reduce_scatter | solution.py:244
  919.0 55.1 %reduce-scatter.15.cloned.1.call-done = f32[128,1024]{1,0:T(8,128)} async-done(((f32[1024,1024]{1,0:T(8,128)}), f32[128,1024]{1,0:T(8,128)}) %reduce-scatter.15.cloned.1.call-update) | async-done | bytes 524304 | tf_op jit(solution)/shard_map/reduce_scatter | solution.py:246
  974.1 55.6 %reduce-scatter.17.cloned.1.call-done = f32[1024,128]{1,0:T(8,128)} async-done(((f32[1024,1024]{1,0:T(8,128)}), f32[1024,128]{1,0:T(8,128)}) %reduce-scatter.17.cloned.1.call-update) | async-done | bytes 524304 | tf_op jit(solution)/shard_map/reduce_scatter | solution.py:247
  (176 shorter events, 27.1 us)
Async XLA Ops:
  7.2 8.5 copy-start
  7.2 10.8 %copy-start.32 = (bf16[128]{0:T(256)(128)(2,1)S(1)}, bf16[128]{0:T(256)(128)(2,1)}, u32[]{:S(2)}) copy-start(bf16[128]{0:T(256)(128)(2,1)} %param.28) | copy-start | bytes 772
  7.2 25.5 %copy-start.33 = (bf16[128]{0:T(256)(128)(2,1)S(1)}, bf16[128]{0:T(256)(128)(2,1)}, u32[]{:S(2)}) copy-start(bf16[128]{0:T(256)(128)(2,1)} %param.29) | copy-start | bytes 772
  7.2 39.3 %copy-start.30 = (bf16[3,256]{1,0:T(4,128)(2,1)S(1)}, bf16[3,256]{1,0:T(4,128)(2,1)}, u32[]{:S(2)}) copy-start(bf16[3,256]{1,0:T(4,128)(2,1)} %param.21) | copy-start | bytes 4612
  7.2 39.9 %copy-start.34 = (s32[1,3]{1,0:T(1,128)S(1)}, s32[1,3]{1,0:T(1,128)}, u32[]{:S(2)}) copy-start(s32[1,3]{1,0:T(1,128)} %param.19) | copy-start | bytes 40
  7.2 40.9 %copy-start.22 = (bf16[256,128]{1,0:T(8,128)(2,1)S(1)}, bf16[256,128]{1,0:T(8,128)(2,1)}, u32[]{:S(2)}) copy-start(bf16[256,128]{1,0:T(8,128)(2,1)} %param.22) | copy-start | bytes 196612
  7.2 66.3 %copy-start.35 = (bf16[128]{0:T(256)(128)(2,1)S(1)}, bf16[128]{0:T(256)(128)(2,1)}, u32[]{:S(2)}) copy-start(bf16[128]{0:T(256)(128)(2,1)} %param.30) | copy-start | bytes 772
  7.3 78.6 %copy-start.36 = (bf16[128]{0:T(256)(128)(2,1)S(1)}, bf16[128]{0:T(256)(128)(2,1)}, u32[]{:S(2)}) copy-start(bf16[128]{0:T(256)(128)(2,1)} %param.31) | copy-start | bytes 772
  7.3 93.0 %copy-start.31 = (bf16[1024]{0:T(1024)(128)(2,1)S(1)}, bf16[1024]{0:T(1024)(128)(2,1)}, u32[]{:S(2)}) copy-start(bf16[1024]{0:T(1024)(128)(2,1)} %param.25) | copy-start | bytes 6148
  7.3 93.6 %copy-start.6 = (bf16[1,3,256,1024]{3,2,1,0:T(8,128)(2,1)S(1)}, bf16[1,3,256,1024]{3,2,1,0:T(8,128)(2,1)}, u32[]{:S(2)}) copy-start(bf16[1,3,256,1024]{3,2,1,0:T(8,128)(2,1)} %param.33) | copy-start | bytes 4718596
  7.3 100.1 %all-gather.10.cloned.1.call-start = ((), (), s32[]{:S(2)}) async-start(), calls=%async_computation.6 | async-start | bytes 1769472 | tf_op jit(solution)/shard_map/all_gather | solution.py:78
  9.2 256.2 %all-gather.12.cloned.1.call-start = ((), (), s32[]{:S(2)}) async-start(), calls=%async_computation.7 | async-start | bytes 2359296 | tf_op jit(solution)/shard_map/all_gather | solution.py:80
  10.0 271.5 %all-gather.14.cloned.1.call-start = ((), (), s32[]{:S(2)}) async-start(), calls=%async_computation.8 | async-start | bytes 2359296 | tf_op jit(solution)/shard_map/all_gather | solution.py:81
  10.7 285.6 %reduce-scatter.7.cloned.1.call-start = ((), (), s32[]{:S(2)}) async-start(), calls=%async_computation.10 | async-start | bytes 1310720 | tf_op jit(solution)/shard_map/reduce_scatter | solution.py:202
  32.7 74.7 %copy-start.20 = (f32[8,1,128]{2,1,0:T(1,128)}, f32[8,1,128]{2,1,0:T(1,128)S(1)}, u32[]{:S(2)}) copy-start(f32[8,1,128]{2,1,0:T(1,128)S(1)} %convert_element_type.144) | copy-start | bytes 12292
  48.1 63.7 %copy-start.16 = (f32[1024,16]{0,1:T(8,128)}, f32[1024,16]{0,1:T(8,128)S(1)}, u32[]{:S(2)}) copy-start(f32[1024,16]{0,1:T(8,128)S(1)} %pad_maximum_fusion.9) | copy-start | bytes 196612
  73.6 29.9 %copy-start.11 = (bf16[256,1024]{1,0:T(8,128)(2,1)}, bf16[256,1024]{1,0:T(8,128)(2,1)S(1)}, u32[]{:S(2)}) copy-start(bf16[256,1024]{1,0:T(8,128)(2,1)S(1)} %all_gather.45) | copy-start | bytes 1572868
  111.7 52.4 %copy-start.13 = (bf16[768,4,64]{0,2,1:T(8,128)(2,1)}, bf16[768,4,64]{0,2,1:T(8,128)(2,1)S(1)}, u32[]{:S(2)}) copy-start(bf16[768,4,64]{0,2,1:T(8,128)(2,1)S(1)} %slice_bitcast_fusion.4) | copy-start | bytes 1179652
  137.6 26.6 %copy-start.18 = (bf16[1024,256]{0,1:T(8,128)(2,1)S(1)}, bf16[1024,256]{0,1:T(8,128)(2,1)}, u32[]{:S(2)}) copy-start(bf16[1024,256]{0,1:T(8,128)(2,1)} %convolution_convert_fusion.2) | copy-start | bytes 1572868
  164.2 22.0 %copy-start.9 = (bf16[1024,256]{0,1:T(8,128)(2,1)}, bf16[1024,256]{0,1:T(8,128)(2,1)S(1)}, u32[]{:S(2)}) copy-start(bf16[1024,256]{0,1:T(8,128)(2,1)S(1)} %all_gather.43) | copy-start | bytes 1572868
  246.8 58.7 %reduce-scatter.9.cloned.1.call-start = ((), (), s32[]{:S(2)}) async-start(), calls=%async_computation.11 | async-start | bytes 1310720 | tf_op jit(solution)/shard_map/reduce_scatter | solution.py:208
  261.2 4.2 copy-start.4
  261.2 4.2 copy-start.26
  261.2 4.3 copy-start.28
  265.2 475.5 %all-reduce.16.cloned.1.call-start = ((), (), s32[]{:S(2)}) async-start(), calls=%async_computation.16 | async-start | bytes 25165824 | tf_op jit(solution)/shard_map/psum | solution.py:158
  265.5 16.0 %copy-start.10 = (bf16[1,256,1024]{2,1,0:T(8,128)(2,1)S(1)}, bf16[1,256,1024]{2,1,0:T(8,128)(2,1)}, u32[]{:S(2)}) copy-start(bf16[1,256,1024]{2,1,0:T(8,128)(2,1)} %param.32) | copy-start | bytes 1572868
  281.5 10.4 %copy-start.39 = (bf16[1024,1024]{1,0:T(8,128)(2,1)S(1)}, bf16[1024,1024]{1,0:T(8,128)(2,1)}, u32[]{:S(2)}) copy-start(bf16[1024,1024]{1,0:T(8,128)(2,1)} %all-gather.12.cloned.1.call-done) | copy-start | bytes 6291460
  291.9 4.4 copy-start.5
  291.9 5.2 copy-start.17
  291.9 5.2 copy-start.19
  296.3 3.8 copy-start.14
  305.5 3.7 copy-start.40
  313.1 516.0 %all-reduce.14.cloned.1.call-start = ((), (), s32[]{:S(2)}) async-start(), calls=%async_computation.9 | async-start | bytes 4194304 | tf_op jit(solution)/shard_map/psum | solution.py:159
  313.3 6.1 copy-start.12
  319.4 562.6 %reduce-scatter.13.cloned.1.call-start = ((), (), s32[]{:S(2)}) async-start(), calls=%async_computation.13 | async-start | bytes 1179648 | tf_op jit(solution)/shard_map/reduce_scatter | solution.py:245
  322.7 596.2 %reduce-scatter.11.cloned.1.call-start = ((), (), s32[]{:S(2)}) async-start(), calls=%async_computation.12 | async-start | bytes 3538944 | tf_op jit(solution)/shard_map/reduce_scatter | solution.py:244
  322.8 5.4 copy-start.29
  328.1 646.0 %reduce-scatter.15.cloned.1.call-start = ((), (), s32[]{:S(2)}) async-start(), calls=%async_computation.14 | async-start | bytes 4718592 | tf_op jit(solution)/shard_map/reduce_scatter | solution.py:246
  334.4 695.3 %reduce-scatter.17.cloned.1.call-start = ((), (), s32[]{:S(2)}) async-start(), calls=%async_computation.15 | async-start | bytes 4718592 | tf_op jit(solution)/shard_map/reduce_scatter | solution.py:247
  340.8 14.3 %copy-start.38 = (bf16[128]{0:T(256)(128)(2,1)S(1)}, bf16[128]{0:T(256)(128)(2,1)}, u32[]{:S(2)}) copy-start(bf16[128]{0:T(256)(128)(2,1)} %param.27) | copy-start | bytes 772
  340.8 27.7 %copy-start.41 = (u32[32]{0:T(128)S(1)}, u32[32]{0:T(128)}, u32[]{:S(2)}) copy-start(u32[32]{0:T(128)} %constant.122) | copy-start | bytes 388
  740.7 4.7 copy-start.24
  829.1 9.3 copy-start.1
  829.1 9.3 copy-start.2
  829.1 9.3 copy-start.7
  838.4 5.4 copy-start.25
  870.4 6.4 copy-start.3
  870.5 159.3 %copy-start.42 = (f32[128]{0:T(128)}, f32[128]{0:T(128)S(1)}, u32[]{:S(2)}) copy-start(f32[128]{0:T(128)S(1)} %dynamic-slice.1) | copy-start | bytes 1540
  (7 other events, 11.7 us)
Sparse Core Ops, SparseCore 0:
  10.6 28.5 all-gather.9
  41.1 33.7 all-gather.11
  76.8 28.1 all-gather.13
  246.9 27.1 reduce-scatter.6
  277.7 27.7 reduce-scatter.8
  313.2 427.4 all-reduce.15
  743.6 85.4 all-reduce.13
  833.1 35.1 reduce-scatter.12
  872.7 46.2 reduce-scatter.10
  922.7 51.3 reduce-scatter.14
  978.4 51.2 reduce-scatter.16
where the time goes:
time: 1050 us; the launch traced here: 1040 us
  waiting for transfers between devices  609 us (58%)
  blocking collectives  159 us (15%)
  matrix products  150 us (14%)
  other arithmetic  76 us (7%)
  local copies, waits for them, and re-layouts  27.1 us (3%)
  between operations  15.5 us (1%)
    psum x1, waiting for transfers between devices, on_device(): attn_total = lax.psum(attn_part, 'tp')  371 us
    psum x1, waiting for transfers between devices, on_device(): lax.psum(mlp_part.astype(jnp.bfloat16), 'tp').astype(jnp.float32)  83.7 us
    reduce_scatter x1, waiting for transfers between devices, on_device(): lax.psum_scatter(grad_down, ('fsdp', 'ctx'), scatter_dimension=1, tiled=T...  55.6 us
    reduce_scatter x1, waiting for transfers between devices, on_device(): lax.psum_scatter(grad_up, ('fsdp', 'ctx'), scatter_dimension=0, tiled=True)  55.1 us
    reduce_scatter x1, waiting for transfers between devices, on_device(): lax.psum_scatter(grad_qkv, ('fsdp', 'ctx'), scatter_dimension=0, tiled=True)  36.9 us
    psum x1, blocking collectives, on_device(): lax.psum((grad_qkv_bias, grad_up_bias), ('fsdp', 'ctx'))  26.6 us
    all_gather x1, blocking collectives, on_device(): lax.all_gather(w_dense, ('fsdp', 'ctx'), axis=1, tiled=True)  25.5 us
    convert_element_type x1, other arithmetic, on_device(): grad_scores = (probs * (grad_probs - inner)).astype(jnp.bfloat16)  24.6 us
  transfers between devices with their start and end apart: 11, of which 6 were waited for; matrix products, arithmetic and copies ran while one was open for 23% of the time, Pallas kernels for 0%

commit v1 on v0

--- a/solution.py
+++ b/solution.py
@@ -6,6 +6,27 @@
 HD = 64
 ROT = 16
 EPS = 1e-05
+
+
+def shape_packet(original, net_axis):
+    tmp = lax.axis_size(net_axis)
+    finding = lax.axis_index(net_axis)
+    frame_out, f_now, all_rows = (tmp, finding, original.shape[1])
+    extra, oldest = (original, 1)
+    while oldest < frame_out:
+        extra = jnp.concatenate(
+            [
+                extra,
+                lax.ppermute(
+                    extra,
+                    net_axis,
+                    list(map(lambda tick: (tick, (tick - oldest) % frame_out), range(frame_out))),
+                ),
+            ],
+            axis=1,
+        )
+        oldest = 2 * oldest
+    return jnp.roll(extra, shift=f_now * all_rows, axis=1)
 
 
 def layer_norm(inputs, norm_gain, norm_shift):
@@ -76,7 +97,7 @@
 ):
     gathered = (
         lax.all_gather(w_qkv, ("fsdp", "ctx"), axis=0, tiled=True),
-        lax.all_gather(w_dense, ("fsdp", "ctx"), axis=1, tiled=True),
+        shape_packet(w_dense, ("fsdp", "ctx")),
         lax.all_gather(w_fc1, ("fsdp", "ctx"), axis=0, tiled=True),
         lax.all_gather(w_fc2, ("fsdp", "ctx"), axis=1, tiled=True),
         lax.all_gather(dense_bias, ("fsdp", "ctx"), axis=0, tiled=True),

time: 1050 us -> 1070 us (1.019)
  transfers between devices with their start and end apart: 11 -> 14, of which waited for: 6 -> 7; matrix products, arithmetic and copies ran while one was open for 23% -> 24% of each run, Pallas kernels for 0% -> 0%
where the time goes in v1:
time: 1070 us; the launch traced here: 1060 us
  waiting for transfers between devices  613 us (57%)
  blocking collectives  158 us (15%)
  matrix products  150 us (14%)
  other arithmetic  77 us (7%)
  local copies, waits for them, and re-layouts  36.6 us (3%)
  between operations  15.5 us (1%)
    psum x1, waiting for transfers between devices, on_device(): attn_total = lax.psum(attn_part, 'tp')  371 us
    psum x1, waiting for transfers between devices, on_device(): lax.psum(mlp_part.astype(jnp.bfloat16), 'tp').astype(jnp.float32)  83.7 us
    reduce_scatter x1, waiting for transfers between devices, on_device(): lax.psum_scatter(grad_down, ('fsdp', 'ctx'), scatter_dimension=1, tiled=T...  55.6 us
    reduce_scatter x1, waiting for transfers between devices, on_device(): lax.psum_scatter(grad_up, ('fsdp', 'ctx'), scatter_dimension=0, tiled=True)  55.1 us
    reduce_scatter x1, waiting for transfers between devices, on_device(): lax.psum_scatter(grad_qkv, ('fsdp', 'ctx'), scatter_dimension=0, tiled=True)  36.9 us
    psum x1, blocking collectives, on_device(): lax.psum((grad_qkv_bias, grad_up_bias), ('fsdp', 'ctx'))  26.6 us
    convert_element_type x1, other arithmetic, on_device(): grad_scores = (probs * (grad_probs - inner)).astype(jnp.bfloat16)  24.6 us
    all_gather x1, blocking collectives, on_device(): lax.all_gather(w_dense, ('fsdp', 'ctx'), axis=1, tiled=True)  23 us
  transfers between devices with their start and end apart: 14, of which 7 were waited for; matrix products, arithmetic and copies ran while one was open for 24% of the time, Pallas kernels for 0%

profile of v1, /device:TPU:0, one launch (start us, length us, event | category | flops | bytes accessed | tf_op | source)
XLA Modules:
  0.0 1056.9 jit_solution(5747467930660462979)
XLA Ops:
  7.3 1.9 copy.36
  10.0 3.4 collective-permute-start
  15.9 23.0 %all_gather.50 = bf16[256,1024]{1,0:T(8,128)(2,1)S(1)} all-gather(bf16[256,128]{1,0:T(8,128)(2,1)} %param.22), channel_id=1, replica_groups=mesh['fsdp'=2,'ctx'=4,'tp'=4] {'fsdp','ctx'}, dimensions={1}, use_global_device_ids=true | all-gather | bytes 589824 | tf_op jit(solution)/shard_map/all_gather | solution.py:185
  38.9 1.9 convert_reduce_fusion
  41.8 2.9 convolution_convert_fusion.2
  44.7 3.8 fusion.2
  48.6 2.2 collective-permute-start.1
  52.1 4.1 collective-permute-done.1
  58.3 13.7 %all-gather = bf16[8,1,128]{2,1,0:T(2,128)(2,1)S(1)} all-gather(bf16[1,1,128]{2,1,0:T(2,128)(2,1)} %bitcast.150), channel_id=1, replica_groups=mesh['fsdp'=2,'ctx'=4,'tp'=4] {'fsdp','ctx'}, dimensions={0}, use_global_device_ids=true | all-gather | bytes 2304 | tf_op jit(solution)/shard_map/all_gather | solution.py:105
  72.0 14.1 %all-gather.1 = bf16[8,1,128]{2,1,0:T(2,128)(2,1)S(1)} all-gather(bf16[1,1,128]{2,1,0:T(2,128)(2,1)} %bitcast.151), channel_id=1, replica_groups=mesh['fsdp'=2,'ctx'=4,'tp'=4] {'fsdp','ctx'}, dimensions={0}, use_global_device_ids=true | all-gather | bytes 2304 | tf_op jit(solution)/shard_map/all_gather | solution.py:106
  88.0 13.3 %all-gather.2 = bf16[8,1,128]{2,1,0:T(2,128)(2,1)S(1)} all-gather(bf16[1,1,128]{2,1,0:T(2,128)(2,1)} %bitcast.152), channel_id=1, replica_groups=mesh['fsdp'=2,'ctx'=4,'tp'=4] {'fsdp','ctx'}, dimensions={0}, use_global_device_ids=true | all-gather | bytes 2304 | tf_op jit(solution)/shard_map/all_gather | solution.py:107
  101.3 14.1 %all-gather.3 = bf16[8,1,128]{2,1,0:T(2,128)(2,1)S(1)} all-gather(bf16[1,1,128]{2,1,0:T(2,128)(2,1)} %bitcast.153), channel_id=1, replica_groups=mesh['fsdp'=2,'ctx'=4,'tp'=4] {'fsdp','ctx'}, dimensions={0}, use_global_device_ids=true | all-gather | bytes 2304 | tf_op jit(solution)/shard_map/all_gather | solution.py:108
  125.7 3.6 convolution_add_fusion
  130.5 13.0 %all_gather.43 = bf16[1024,256]{0,1:T(8,128)(2,1)S(1)} all-gather(bf16[256,256]{0,1:T(8,128)(2,1)S(1)} %bitcast.130), channel_id=1, replica_groups=mesh['fsdp'=2,'ctx'=4,'tp'=4] {'ctx'}, dimensions={0}, use_global_device_ids=true | all-gather | bytes 655360 | tf_op jit(solution)/shard_map/all_gather | solution.py:156
  143.5 12.8 %fusion = (f32[4,1024]{1,0:T(4,128)S(1)}, f32[4,1024,1792]{2,1,0:T(8,128)}) fusion(pred[1024,1792]{1,0:T(8,128)(4,1)S(1)} %fusion.2, bf16[1024,4,48]{0,2,1:T(8,128)(2,1)S(1)} %slice.216, bf16[1024,4,16]{0,2,1:T(8,128)(2,1)S(1)} %get-tuple-element.57, bf16[1024,4,64]{0,2,1:T(8,128)(2,1)S(1)} %bitcast.122, bf16[1024,4,48]{0,2,1:T(8,128)(2,1)S(1)} %slice.217, ...), kind=kOutput, calls=%fused_computation.5 | convolution fusion | flops 966717440 | bytes 32784384 | tf_op jit(solution)/shard_map/qhd,khd->hqk/dot_general | solution.py:69
  156.4 13.8 %exponential_reduce_fusion = f32[4,1024]{1,0:T(4,128)S(1)} fusion(f32[4,1024,1792]{2,1,0:T(8,128)} %get-tuple-element.66, f32[4,1024]{1,0:T(4,128)S(1)} %get-tuple-element.65, pred[1024,1792]{1,0:T(8,128)(4,1)S(1)} %fusion.2), kind=kLoop, calls=%fused_computation.3 | loop fusion | flops 29356032 | bytes 31227904 | tf_op jit(solution)/shard_map/reduce_sum | solution.py:169
  170.2 13.4 %all_gather.42 = bf16[1024,256]{0,1:T(8,128)(2,1)S(1)} all-gather(bf16[256,256]{0,1:T(8,128)(2,1)S(1)} %bitcast.131), channel_id=1, replica_groups=mesh['fsdp'=2,'ctx'=4,'tp'=4] {'ctx'}, dimensions={0}, use_global_device_ids=true | all-gather | bytes 655360 | tf_op jit(solution)/shard_map/all_gather | solution.py:157
  183.6 22.0 %multiply_reduce_fusion = (f32[4,1024]{1,0:T(4,128)S(1)}, f32[4,1024,1792]{2,1,0:T(8,128)}) fusion(f32[4,1024,1792]{2,1,0:T(8,128)} %get-tuple-element.66, f32[4,1024]{1,0:T(4,128)S(1)} %log_add_fusion, pred[1024,1792]{1,0:T(8,128)(4,1)S(1)} %fusion.2, bf16[1024,4,64]{0,2,1:T(8,128)(2,1)S(1)} %bitcast.128, bf16[768,4,64]{0,2,1:T(8,128)(2,1)S(1)} %slice_bitcast_fusion.4, ...), kind=kOutput, calls=%fused_computation.1 | convolution fusion | flops 978055168 | bytes 62029824 | tf_op jit(solution)/shard_map/qhd,khd->hqk/dot_general | solution.py:207
  205.6 24.6 %multiply_convert_fusion = bf16[4,1024,1792]{2,1,0:T(8,128)(2,1)} fusion(f32[4,1024,1792]{2,1,0:T(8,128)} %get-tuple-element.69, f32[4,1024,1792]{2,1,0:T(8,128)} %get-tuple-element.66, f32[4,1024]{1,0:T(4,128)S(1)} %get-tuple-element.68, f32[4,1024]{1,0:T(4,128)S(1)} %log_add_fusion, pred[1024,1792]{1,0:T(8,128)(4,1)S(1)} %fusion.2), kind=kLoop, calls=%fused_computation | loop fusion | flops 44040192 | bytes 75268096 | tf_op jit(solution)/shard_map/convert_element_type | solution.py:211
  230.2 7.8 fusion.30
  240.1 12.7 %convolution_bitcast_fusion = f32[1792,4,64]{0,2,1:T(8,128)S(1)} fusion(bf16[1024,4,64]{0,2,1:T(8,128)(2,1)S(1)} %bitcast.129, f32[4,1024,1792]{2,1,0:T(8,128)} %get-tuple-element.66, f32[4,1024]{1,0:T(4,128)S(1)} %log_add_fusion, pred[1024,1792]{1,0:T(8,128)(4,1)S(1)} %fusion.2), kind=kOutput, calls=%fused_computation.58 | convolution fusion | flops 968884224 | bytes 33570816 | tf_op jit(solution)/shard_map/hqk,qhd->khd/dot_general | solution.py:219
  254.7 9.7 fusion.35
  266.3 14.3 %convolution_convert_fusion.1 = bf16[4,64,1024]{2,1,0:T(8,128)(2,1)} fusion(bf16[768,4,64]{0,2,1:T(8,128)(2,1)} %copy-done.13, bf16[1024,4,64]{0,2,1:T(8,128)(2,1)} %bitcast.116, f32[4,1024,1792]{2,1,0:T(8,128)} %get-tuple-element.66, f32[4,1024]{1,0:T(4,128)S(1)} %log_add_fusion, pred[1024,1792]{1,0:T(8,128)(4,1)S(1)} %fusion.2), kind=kOutput, calls=%fused_computation.75 | convolution fusion | flops 970981376 | bytes 32653312 | tf_op jit(solution)/shard_map/hqk,khd->qhd/dot_general | solution.py:171
  280.9 3.9 fusion.42
  284.8 16.0 %multiply_convert_fusion.1 = (bf16[1024,1024]{1,0:T(8,128)(2,1)}, f32[1024,1024]{1,0:T(8,128)}, f32[1024,1024]{1,0:T(8,128)}) fusion(f32[1024]{0:T(1024)S(1)} %copy-done.28, bf16[1024,1024]{1,0:T(8,128)(2,1)} %all-gather.12.cloned.1.call-done, f32[1024]{0:T(1024)S(1)} %bitcast.147, f32[1024]{0:T(1024)S(1)} %bitcast.138, f32[1024]{0:T(1024)S(1)} %fusion.57, ...), kind=kOutput, calls=%fused_computation.41 | convolution fusion | flops 2226126848 | bytes 14700544 | tf_op jit(solution)/shard_map/dot_general | solution.py:174
  300.9 9.1 convert_reduce_fusion.2
  311.3 4.4 fusion.81
  319.6 5.6 reduce-scatter.9.cloned.1.call-done
  328.9 3.8 fusion.82
  333.0 6.0 convolution_convert_fusion
  339.1 3.3 fusion.76
  342.5 5.3 fusion.31
  347.9 6.2 fusion.67
  354.1 6.4 fusion.75
  361.1 13.6 %all-gather.4 = bf16[8,1,128]{2,1,0:T(2,128)(2,1)S(1)} all-gather(bf16[1,1,128]{2,1,0:T(2,128)(2,1)S(1)} %bitcast.154), channel_id=1, replica_groups=mesh['fsdp'=2,'ctx'=4,'tp'=4] {'fsdp','ctx'}, dimensions={0}, use_global_device_ids=true | all-gather | bytes 2304 | tf_op jit(solution)/shard_map/all_gather | solution.py:103
  374.8 13.4 %all-gather.5 = bf16[8,1,128]{2,1,0:T(2,128)(2,1)S(1)} all-gather(bf16[1,1,128]{2,1,0:T(2,128)(2,1)S(1)} %bitcast.155), channel_id=1, replica_groups=mesh['fsdp'=2,'ctx'=4,'tp'=4] {'fsdp','ctx'}, dimensions={0}, use_global_device_ids=true | all-gather | bytes 2304 | tf_op jit(solution)/shard_map/all_gather | solution.py:104
  389.5 370.9 %all-reduce.16.cloned.1.call-done = (f32[1024,1024]{1,0:T(8,128)}, f32[1024,1024]{1,0:T(8,128)}, f32[1024,1024]{1,0:T(8,128)}) async-done(((f32[1024,1024]{1,0:T(8,128)}, f32[1024,1024]{1,0:T(8,128)}, f32[1024,1024]{1,0:T(8,128)}), (f32[1024,1024]{1,0:T(8,128)}, f32[1024,1024]{1,0:T(8,128)}, f32[1024,1024]{1,0:T(8,128)})) %all-reduce.16.cloned.1.call-update) | async-done | bytes 12582928 | tf_op jit(solution)/shard_map/psum | solution.py:179
  760.4 4.7 fusion.79
  765.1 83.7 %all-reduce.14.cloned.1.call-done = bf16[1024,1024]{1,0:T(8,128)(2,1)} async-done(((bf16[1024,1024]{1,0:T(8,128)(2,1)}), bf16[1024,1024]{1,0:T(8,128)(2,1)}) %all-reduce.14.cloned.1.call-update) | async-done | bytes 2097168 | tf_op jit(solution)/shard_map/psum | solution.py:180
  848.8 9.3 fusion.18
  858.1 5.4 convert_reduce_fusion.1
  863.5 26.6 %all-reduce.9 = (f32[3,256]{1,0:T(4,128)}, f32[1024]{0:T(1024)S(1)}, f32[1024]{0:T(1024)}, f32[1024]{0:T(1024)S(1)}, f32[1024]{0:T(1024)S(1)}, /*index=5*/f32[1024]{0:T(1024)S(1)}, f32[1024]{0:T(1024)S(1)}) all-reduce(f32[3,256]{1,0:T(4,128)S(1)} %reshape.336, ...), channel_id=1, replica_groups=mesh['fsdp'=2,'ctx'=4,'tp'=4] {'fsdp','ctx'}, use_global_device_ids=true, to_apply=%region_17.18 | all-reduce | flops 6912 | bytes 55296 | tf_op jit(solution)/shard_map/psum | solution.py:275
  892.5 4.0 slice.168
  896.4 1.9 slice.152
  898.3 2.3 slice_bitcast_fusion
  901.7 36.9 %reduce-scatter.11.cloned.1.call-done = f32[128,3,256]{2,0,1:T(8,128)} async-done(((f32[1024,3,256]{2,0,1:T(8,128)}), f32[128,3,256]{2,0,1:T(8,128)}) %reduce-scatter.11.cloned.1.call-update) | async-done | bytes 393232 | tf_op jit(solution)/shard_map/reduce_scatter | solution.py:265
  938.6 55.1 %reduce-scatter.15.cloned.1.call-done = f32[128,1024]{1,0:T(8,128)} async-done(((f32[1024,1024]{1,0:T(8,128)}), f32[128,1024]{1,0:T(8,128)}) %reduce-scatter.15.cloned.1.call-update) | async-done | bytes 524304 | tf_op jit(solution)/shard_map/reduce_scatter | solution.py:267
  993.8 55.6 %reduce-scatter.17.cloned.1.call-done = f32[1024,128]{1,0:T(8,128)} async-done(((f32[1024,1024]{1,0:T(8,128)}), f32[1024,128]{1,0:T(8,128)}) %reduce-scatter.17.cloned.1.call-update) | async-done | bytes 524304 | tf_op jit(solution)/shard_map/reduce_scatter | solution.py:268
  (184 shorter events, 41.9 us)
Async XLA Ops:
  7.2 33.5 %copy-start.4 = (bf16[1,256,1024]{2,1,0:T(8,128)(2,1)S(1)}, bf16[1,256,1024]{2,1,0:T(8,128)(2,1)}, u32[]{:S(2)}) copy-start(bf16[1,256,1024]{2,1,0:T(8,128)(2,1)} %param.17) | copy-start | bytes 1572868
  7.2 33.5 %copy-start = (bf16[1,3,256,1024]{3,2,1,0:T(8,128)(2,1)S(1)}, bf16[1,3,256,1024]{3,2,1,0:T(8,128)(2,1)}, u32[]{:S(2)}) copy-start(bf16[1,3,256,1024]{3,2,1,0:T(8,128)(2,1)} %param.18) | copy-start | bytes 4718596
  7.2 34.3 %copy-start.32 = (s32[1,3]{1,0:T(1,128)S(1)}, s32[1,3]{1,0:T(1,128)}, u32[]{:S(2)}) copy-start(s32[1,3]{1,0:T(1,128)} %param.19) | copy-start | bytes 40
  7.2 34.6 %copy-start.10 = (bf16[1,256,1024]{2,1,0:T(8,128)(2,1)S(1)}, bf16[1,256,1024]{2,1,0:T(8,128)(2,1)}, u32[]{:S(2)}) copy-start(bf16[1,256,1024]{2,1,0:T(8,128)(2,1)} %param.32) | copy-start | bytes 1572868
  7.2 118.5 %all-gather.10.cloned.1.call-start = ((), (), s32[]{:S(2)}) async-start(), calls=%async_computation.6 | async-start | bytes 1769472 | tf_op jit(solution)/shard_map/all_gather | solution.py:99
  9.2 275.6 %all-gather.12.cloned.1.call-start = ((), (), s32[]{:S(2)}) async-start(), calls=%async_computation.7 | async-start | bytes 2359296 | tf_op jit(solution)/shard_map/all_gather | solution.py:101
  9.9 290.9 %all-gather.14.cloned.1.call-start = ((), (), s32[]{:S(2)}) async-start(), calls=%async_computation.8 | async-start | bytes 2359296 | tf_op jit(solution)/shard_map/all_gather | solution.py:102
  10.0 38.6 %collective-permute-start = (bf16[256,128]{1,0:T(8,128)(2,1)}, bf16[256,128]{1,0:T(8,128)(2,1)S(1)}, u32[]{:S(2)}, u32[]{:S(2)}) collective-permute-start(bf16[256,128]{1,0:T(8,128)(2,1)} %param.22), channel_id=1, source_target_pairs={{0,28},{4,0},{8,4},{12,8},{16,12},{20,16},{24,20},{28,24},{1,29},{... | collective-permute-start | bytes 196616 | tf_op jit(solution)/shard_map/ppermute | solution.py:20
  13.4 302.3 %reduce-scatter.7.cloned.1.call-start = ((), (), s32[]{:S(2)}) async-start(), calls=%async_computation.10 | async-start | bytes 1310720 | tf_op jit(solution)/shard_map/reduce_scatter | solution.py:223
  41.4 16.2 %copy-start.25 = (f32[1024]{0:T(1024)}, f32[1024]{0:T(1024)S(1)}, u32[]{:S(2)}) copy-start(f32[1024]{0:T(1024)S(1)} %fusion.19) | copy-start | bytes 12292
  41.4 7.1 copy-start.12
  48.6 7.6 collective-permute-start.1
  57.6 61.9 %collective-permute-start.2 = (bf16[256,512]{1,0:T(8,128)(2,1)}, bf16[256,512]{1,0:T(8,128)(2,1)}, u32[]{:S(2)}, u32[]{:S(2)}) collective-permute-start(bf16[256,512]{1,0:T(8,128)(2,1)} %pad_maximum_fusion.8), channel_id=1, source_target_pairs={{0,16},{4,20},{8,24},{12,28},{16,0},{20,4},{24,8},{28,12},{1,17},{... | collective-permute-start | bytes 786440 | tf_op jit(solution)/shard_map/ppermute | solution.py:20
  72.0 57.3 %copy-start.23 = (f32[8,1,128]{2,1,0:T(1,128)}, f32[8,1,128]{2,1,0:T(1,128)S(1)}, u32[]{:S(2)}) copy-start(f32[8,1,128]{2,1,0:T(1,128)S(1)} %convert_element_type.144) | copy-start | bytes 12292
  130.0 53.5 %copy-start.13 = (bf16[768,4,64]{0,2,1:T(8,128)(2,1)}, bf16[768,4,64]{0,2,1:T(8,128)(2,1)S(1)}, u32[]{:S(2)}) copy-start(bf16[768,4,64]{0,2,1:T(8,128)(2,1)S(1)} %slice_bitcast_fusion.4) | copy-start | bytes 1179652
  156.3 27.2 %copy-start.20 = (bf16[1024,256]{0,1:T(8,128)(2,1)S(1)}, bf16[1024,256]{0,1:T(8,128)(2,1)}, u32[]{:S(2)}) copy-start(bf16[1024,256]{0,1:T(8,128)(2,1)} %convolution_convert_fusion.2) | copy-start | bytes 1572868
  183.6 22.0 %copy-start.9 = (bf16[1024,256]{0,1:T(8,128)(2,1)}, bf16[1024,256]{0,1:T(8,128)(2,1)S(1)}, u32[]{:S(2)}) copy-start(bf16[1024,256]{0,1:T(8,128)(2,1)S(1)} %all_gather.42) | copy-start | bytes 1572868
  266.3 58.9 %reduce-scatter.9.cloned.1.call-start = ((), (), s32[]{:S(2)}) async-start(), calls=%async_computation.11 | async-start | bytes 1310720 | tf_op jit(solution)/shard_map/reduce_scatter | solution.py:229
  280.7 4.2 copy-start.5
  280.7 4.2 copy-start.28
  280.7 4.2 copy-start.30
  280.7 479.7 %all-reduce.16.cloned.1.call-start = ((), (), s32[]{:S(2)}) async-start(), calls=%async_computation.16 | async-start | bytes 25165824 | tf_op jit(solution)/shard_map/psum | solution.py:179
  284.8 16.0 %copy-start.11 = (bf16[1,256,1024]{2,1,0:T(8,128)(2,1)S(1)}, bf16[1,256,1024]{2,1,0:T(8,128)(2,1)}, u32[]{:S(2)}) copy-start(bf16[1,256,1024]{2,1,0:T(8,128)(2,1)} %param.32) | copy-start | bytes 1572868
  300.9 10.4 copy-start.35
  310.0 1.3 copy-start.39
  311.3 4.4 copy-start.6
  311.3 5.2 copy-start.19
  311.3 5.3 copy-start.21
  315.7 3.8 copy-start.14
  325.2 3.7 copy-start.36
  332.7 516.0 %all-reduce.14.cloned.1.call-start = ((), (), s32[]{:S(2)}) async-start(), calls=%async_computation.9 | async-start | bytes 4194304 | tf_op jit(solution)/shard_map/psum | solution.py:180
  333.0 6.1 copy-start.16
  339.0 3.4 copy-start.24
  339.0 3.5 copy-start.29
  339.0 562.7 %reduce-scatter.13.cloned.1.call-start = ((), (), s32[]{:S(2)}) async-start(), calls=%async_computation.13 | async-start | bytes 1179648 | tf_op jit(solution)/shard_map/reduce_scatter | solution.py:266
  342.4 596.2 %reduce-scatter.11.cloned.1.call-start = ((), (), s32[]{:S(2)}) async-start(), calls=%async_computation.12 | async-start | bytes 3538944 | tf_op jit(solution)/shard_map/reduce_scatter | solution.py:265
  342.5 5.4 copy-start.31
  347.8 646.0 %reduce-scatter.15.cloned.1.call-start = ((), (), s32[]{:S(2)}) async-start(), calls=%async_computation.14 | async-start | bytes 4718592 | tf_op jit(solution)/shard_map/reduce_scatter | solution.py:267
  354.1 695.4 %reduce-scatter.17.cloned.1.call-start = ((), (), s32[]{:S(2)}) async-start(), calls=%async_computation.15 | async-start | bytes 4718592 | tf_op jit(solution)/shard_map/reduce_scatter | solution.py:268
  360.5 14.3 %copy-start.34 = (bf16[128]{0:T(256)(128)(2,1)S(1)}, bf16[128]{0:T(256)(128)(2,1)}, u32[]{:S(2)}) copy-start(bf16[128]{0:T(256)(128)(2,1)} %param.27) | copy-start | bytes 772
  360.5 27.7 %copy-start.37 = (u32[32]{0:T(128)S(1)}, u32[32]{0:T(128)}, u32[]{:S(2)}) copy-start(u32[32]{0:T(128)} %constant.152) | copy-start | bytes 388
  760.4 4.7 copy-start.26
  848.8 9.3 copy-start.1
  848.8 9.3 copy-start.2
  848.8 9.3 copy-start.7
  858.1 5.4 copy-start.27
  890.1 6.4 copy-start.3
  890.1 159.3 %copy-start.38 = (f32[128]{0:T(128)}, f32[128]{0:T(128)S(1)}, u32[]{:S(2)}) copy-start(f32[128]{0:T(128)S(1)} %dynamic-slice.1) | copy-start | bytes 1540
  (6 other events, 5.3 us)
Sparse Core Ops, SparseCore 0:
  10.5 32.4 all-gather.9
  44.9 28.5 all-gather.11
  75.3 28.2 all-gather.13
  266.4 27.4 reduce-scatter.6
  297.4 27.7 reduce-scatter.8
  332.9 427.4 all-reduce.15
  763.3 85.4 all-reduce.13
  852.8 35.1 reduce-scatter.12
  892.4 46.2 reduce-scatter.10
  942.4 51.3 reduce-scatter.14
  998.1 51.2 reduce-scatter.16
